TPU v7x, 32 devices: a whole 2x2x4 slice. The times are simulated.
32 devices in a mesh: section: 2 (over x), gy: 4 (over y, core), gx: 4 (over z).
Axes of the slice: x: 2, y: 2, z: 4, core: 2. Of those that a mesh axis runs over, the one named last changes fastest.
Arguments:
- images: bfloat16 [2, 128, 256, 128], P('section', 'gy', 'gx'), may hold values from -6 to 6
- first_kernel: bfloat16 [3, 3, 128, 128], replicated, may hold values from -0.1875 to 0.1875
- projection: bfloat16 [128, 256], replicated, may hold values from -0.5 to 0.5
- second_kernel: bfloat16 [3, 3, 256, 256], replicated, may hold values from -0.125 to 0.125
- cotangent: bfloat16 [2, 64, 128, 256], P('section', 'gy', 'gx'), may hold values from -0.625 to 0.625
Outputs:
- features: bfloat16 [2, 64, 128, 256], P('section', 'gy', 'gx')
- grad_first: float32 [3, 3, 128, 128], replicated
- grad_projection: float32 [128, 256], replicated
- grad_second: float32 [3, 3, 256, 256], replicated
All inputs are finite; a program needn't handle non-finite values.
Results may differ from a plain program's by a relative error of at most 0.014.
Values may be sent and summed in bfloat16 or wider, within the bound.
No kernel may reach another device: no remote copies, remote signals or barrier semaphores. Data moves between devices by JAX's collectives and lax.ppermute only.
A program may use at most 64 MiB of HBM per device.

v0:
```python
import jax
import jax.numpy as jnp
from jax import lax
from jax.sharding import PartitionSpec as P


def padded_2(array, sides, width):
    for axis, dim in sides:
        size, length = (lax.axis_size(axis), array.shape[dim])
        up = [(i, (i + 1) % size) for i in range(size - 1)]
        down = [(j, i) for i, j in up]
        last = lax.slice_in_dim(array, length - width, length, axis=dim)
        initial = lax.slice_in_dim(array, 0, width, axis=dim)
        before = lax.ppermute(last, axis, up)
        after = lax.ppermute(initial, axis, down)
        array = jnp.concatenate([before, array, after], axis=dim)
    return array


def from_partner(block, axis, bit):
    count = lax.axis_size(axis)
    route = []
    for low in range(count):
        high = low | 1 << bit
        if high != low and high < count:
            route += [(low, high), (high, low)]
    return lax.ppermute(block, axis, route)


def silu_slope(values):
    sigma = jax.nn.sigmoid(values)
    return sigma * (1.0 + values * (1.0 - sigma))


def conv_forward(padded, kernel, row_count, col_count):
    total = jnp.zeros((row_count * col_count, kernel.shape[3]), jnp.float32)
    for row_tap in range(3):
        for col_tap in range(3):
            piece = padded[row_tap : row_tap + row_count, col_tap : col_tap + col_count].reshape(
                row_count * col_count, padded.shape[2]
            )
            total = total + jnp.dot(
                piece, kernel[row_tap, col_tap], preferred_element_type=jnp.float32
            )
    return total


def conv_slopes(padded, slope, row_count, col_count):
    pieces = []
    for row_tap in range(3):
        for col_tap in range(3):
            piece = padded[row_tap : row_tap + row_count, col_tap : col_tap + col_count].reshape(
                row_count * col_count, padded.shape[2]
            )
            pieces.append(jnp.einsum("pc,pd->cd", piece, slope, preferred_element_type=jnp.float32))
    return jnp.stack(pieces).reshape(3, 3, padded.shape[2], slope.shape[1])


def conv_back(padded, kernel, row_count, col_count):
    total = jnp.zeros((row_count * col_count, kernel.shape[2]), jnp.float32)
    for row_tap in range(3):
        for col_tap in range(3):
            piece = padded[
                2 - row_tap : 2 - row_tap + row_count, 2 - col_tap : 2 - col_tap + col_count
            ].reshape(row_count * col_count, padded.shape[2])
            total = total + jnp.einsum(
                "pd,cd->pc", piece, kernel[row_tap, col_tap], preferred_element_type=jnp.float32
            )
    return total


def first_forward(tile, first_kernel):
    row_count, col_count, channels = tile.shape
    padded = padded_2(tile, (("gy", 0), ("gx", 1)), 1)
    before = conv_forward(padded, first_kernel, row_count, col_count)
    hidden = jax.nn.silu(before).astype(jnp.bfloat16).reshape(row_count, col_count, channels)
    pooled = (
        hidden.astype(jnp.float32)
        .reshape(row_count // 2, 2, col_count // 2, 2, channels)
        .sum(axis=(1, 3))
        * 0.25
    ).astype(jnp.bfloat16)
    return (padded, before, pooled)


def project(pooled, projection):
    half_rows, half_cols, channels = pooled.shape
    flat = jnp.dot(
        pooled.reshape(half_rows * half_cols, channels),
        projection,
        preferred_element_type=jnp.float32,
    )
    return flat.astype(jnp.bfloat16).reshape(half_rows, half_cols, projection.shape[1])


def second_pass(middle, second_kernel, upstream):
    half_rows, half_cols, wide = middle.shape
    padded = padded_2(middle, (("gy", 0), ("gx", 1)), 1)
    before = conv_forward(padded, second_kernel, half_rows, half_cols)
    output = jax.nn.silu(before).astype(jnp.bfloat16).reshape(half_rows, half_cols, wide)
    flat_up = upstream.reshape(half_rows * half_cols, wide).astype(jnp.float32)
    slope = (flat_up * silu_slope(before)).astype(jnp.bfloat16)
    kernel_grad = conv_slopes(padded, slope, half_rows, half_cols)
    slope_padded = padded_2(slope.reshape(half_rows, half_cols, wide), (("gy", 0), ("gx", 1)), 1)
    back = conv_back(slope_padded, second_kernel, half_rows, half_cols).astype(jnp.bfloat16)
    return (output, kernel_grad, back.reshape(half_rows, half_cols, wide))


def projection_back(pooled, back, projection):
    half_rows, half_cols, channels = pooled.shape
    flat_pool = pooled.reshape(half_rows * half_cols, channels)
    flat_back = back.reshape(half_rows * half_cols, back.shape[2])
    grad = jnp.einsum("pc,pd->cd", flat_pool, flat_back, preferred_element_type=jnp.float32)
    pooled_slope = jnp.einsum(
        "pd,cd->pc", flat_back, projection, preferred_element_type=jnp.float32
    )
    return (grad, pooled_slope.astype(jnp.bfloat16).reshape(half_rows, half_cols, channels))


def first_back(padded, before, pooled_slope):
    half_rows, half_cols, channels = pooled_slope.shape
    spread = jnp.broadcast_to(
        (pooled_slope.astype(jnp.float32) * 0.25)[:, None, :, None, :],
        (half_rows, 2, half_cols, 2, channels),
    )
    spread = spread.reshape(4 * half_rows * half_cols, channels)
    slope = (spread * silu_slope(before)).astype(jnp.bfloat16)
    return conv_slopes(padded, slope, 2 * half_rows, 2 * half_cols)


def per_device(images, first_kernel, projection, second_kernel, cotangent):
    padded, before, pooled = first_forward(images[0], first_kernel)
    upstream = from_partner(cotangent[0], "section", 0)
    middle = project(pooled, projection)
    output, grad_second, back = second_pass(middle, second_kernel, upstream)
    grad_projection, pooled_slope = projection_back(pooled, back, projection)
    output = from_partner(output, "section", 0)
    grad_first = first_back(padded, before, pooled_slope)
    grad_first, grad_projection, grad_second = lax.psum(
        (grad_first, grad_projection, grad_second), ("section", "gy", "gx")
    )
    return (output[None], grad_first, grad_projection, grad_second)


def solution(mesh):
    placed = (P("section", "gy", "gx", None), P(), P(), P(), P("section", "gy", "gx", None))
    return jax.shard_map(
        per_device,
        mesh=mesh,
        in_specs=placed,
        out_specs=(P("section", "gy", "gx", None), P(), P(), P()),
        check_vma=False,
    )
```

profile of v0, /device:TPU:0, one launch (start us, length us, event | category | flops | bytes accessed | tf_op | source)
XLA Modules:
  0.0 227.4 jit_solution(3787896188777336523)
XLA Ops:
  7.2 0.8 slice_bitcast_fusion.5
  8.0 2.4 %collective-permute-start = (bf16[1,64,128]{2,1,0:T(8,128)(2,1)S(1)}, bf16[1,64,128]{2,1,0:T(8,128)(2,1)S(1)}, u32[]{:S(2)}, u32[]{:S(2)}) collective-permute-start(bf16[1,64,128]{2,1,0:T(8,128)(2,1)S(1)} %get-tuple-element.21), channel_id=1, source_target_pairs={{0,4},{4,8},{8,12},{1,5},{5,9},{9,13},{2,6},{6,10},{10,14},{3,7},{... | collective-permute-start | bytes 49160 | tf_op jit(solution)/shard_map/ppermute | solution.py:14
  10.4 1.3 collective-permute-start.1
  11.7 3.9 %collective-permute-done.1 = bf16[1,64,128]{2,1,0:T(8,128)(2,1)S(1)} collective-permute-done((bf16[1,64,128]{2,1,0:T(8,128)(2,1)S(1)}, bf16[1,64,128]{2,1,0:T(8,128)(2,1)S(1)}, u32[]{:S(2)}, u32[]{:S(2)}) %collective-permute-start.1) | collective-permute-done | bytes 16416 | tf_op jit(solution)/shard_map/ppermute | solution.py:15
  15.6 0.9 pad_maximum_fusion.17
  16.5 3.5 %collective-permute-start.2 = (bf16[34,1,128]{2,1,0:T(2,128)(2,1)S(1)}, bf16[34,1,128]{2,1,0:T(2,128)(2,1)S(1)}, u32[]{:S(2)}, u32[]{:S(2)}) collective-permute-start(bf16[34,1,128]{2,1,0:T(2,128)(2,1)S(1)} %get-tuple-element.15), channel_id=1, source_target_pairs={{0,1},{1,2},{2,3},{4,5},{5,6},{6,7},{8,9},{9,10},{10,11},{12,13},{... | collective-permute-start | bytes 26120 | tf_op jit(solution)/shard_map/ppermute | solution.py:14
  20.0 1.4 collective-permute-start.3
  21.5 1.3 pad_maximum_fusion.1
  23.1 2.8 %collective-permute-done.3 = bf16[34,1,128]{2,1,0:T(2,128)(2,1)S(1)} collective-permute-done((bf16[34,1,128]{2,1,0:T(2,128)(2,1)S(1)}, bf16[34,1,128]{2,1,0:T(2,128)(2,1)S(1)}, u32[]{:S(2)}, u32[]{:S(2)}) %collective-permute-start.3) | collective-permute-done | bytes 8736 | tf_op jit(solution)/shard_map/ppermute | solution.py:15
  26.2 0.6 fusion.85
  29.3 0.9 convert_reduce_fusion
  30.4 3.0 %collective-permute-start.4 = (bf16[1,32,256]{2,1,0:T(8,128)(2,1)S(1)}, bf16[1,32,256]{2,1,0:T(8,128)(2,1)S(1)}, u32[]{:S(2)}, u32[]{:S(2)}) collective-permute-start(bf16[1,32,256]{2,1,0:T(8,128)(2,1)S(1)} %get-tuple-element.49), channel_id=1, source_target_pairs={{0,4},{4,8},{8,12},{1,5},{5,9},{9,13},{2,6},{6,10},{10,14},{3,7},{... | collective-permute-start | bytes 49160 | tf_op jit(solution)/shard_map/ppermute | solution.py:14
  33.4 1.3 collective-permute-start.5
  34.7 1.6 collective-permute-start.9
  36.3 1.2 collective-permute-done.5
  37.5 3.5 %collective-permute-start.6 = (bf16[18,1,256]{2,1,0:T(2,128)(2,1)S(1)}, bf16[18,1,256]{2,1,0:T(2,128)(2,1)S(1)}, u32[]{:S(2)}, u32[]{:S(2)}) collective-permute-start(bf16[18,1,256]{2,1,0:T(2,128)(2,1)S(1)} %get-tuple-element.41), channel_id=1, source_target_pairs={{0,1},{1,2},{2,3},{4,5},{5,6},{6,7},{8,9},{9,10},{10,11},{12,13},{... | collective-permute-start | bytes 27656 | tf_op jit(solution)/shard_map/ppermute | solution.py:14
  40.9 1.3 collective-permute-start.7
  42.5 4.1 %collective-permute-done.7 = bf16[18,1,256]{2,1,0:T(2,128)(2,1)S(1)} collective-permute-done((bf16[18,1,256]{2,1,0:T(2,128)(2,1)S(1)}, bf16[18,1,256]{2,1,0:T(2,128)(2,1)S(1)}, u32[]{:S(2)}, u32[]{:S(2)}) %collective-permute-start.7) | collective-permute-done | bytes 9248 | tf_op jit(solution)/shard_map/ppermute | solution.py:15
  49.4 3.2 %collective-permute-start.10 = (bf16[1,32,256]{2,1,0:T(8,128)(2,1)S(1)}, bf16[1,32,256]{2,1,0:T(8,128)(2,1)S(1)}, u32[]{:S(2)}, u32[]{:S(2)}) collective-permute-start(bf16[1,32,256]{2,1,0:T(8,128)(2,1)S(1)} %get-tuple-element.45), channel_id=1, source_target_pairs={{0,4},{4,8},{8,12},{1,5},{5,9},{9,13},{2,6},{6,10},{10,14},{3,7},{... | collective-permute-start | bytes 49160 | tf_op jit(solution)/shard_map/ppermute | solution.py:14
  52.6 1.3 collective-permute-start.11
  56.5 1.3 collective-permute-start.12
  57.8 4.7 %collective-permute-start.13 = (bf16[18,1,256]{2,1,0:T(2,128)(2,1)S(1)}, bf16[18,1,256]{2,1,0:T(2,128)(2,1)S(1)}, u32[]{:S(2)}, u32[]{:S(2)}) collective-permute-start(bf16[18,1,256]{2,1,0:T(2,128)(2,1)S(1)} %get-tuple-element.38), channel_id=1, source_target_pairs={{0,1},{1,2},{2,3},{4,5},{5,6},{6,7},{8,9},{9,10},{10,11},{12,13},{... | collective-permute-start | bytes 27656 | tf_op jit(solution)/shard_map/ppermute | solution.py:14
  62.9 0.9 collective-permute-done.13
  66.4 0.9 fusion.91
  71.6 0.8 copy-done.4
  72.5 1.4 collective-permute-start.8
  73.9 7.5 %collective-permute-done.8 = bf16[16,32,256]{2,1,0:T(8,128)(2,1)S(1)} collective-permute-done((bf16[16,32,256]{2,1,0:T(8,128)(2,1)S(1)}, bf16[16,32,256]{2,1,0:T(8,128)(2,1)S(1)}, u32[]{:S(2)}, u32[]{:S(2)}) %collective-permute-start.8) | collective-permute-done | bytes 262176 | tf_op jit(solution)/shard_map/ppermute | solution.py:27
  81.3 132.7 %all-reduce.3.cloned.1.call-done = (f32[3,3,128,128]{3,2,1,0:T(8,128)}, f32[128,256]{1,0:T(8,128)}, f32[3,3,256,256]{3,2,1,0:T(8,128)}) async-done(((f32[3,3,128,128]{3,2,1,0:T(8,128)}, f32[128,256]{1,0:T(8,128)}, f32[3,3,256,256]{3,2,1,0:T(8,128)}), (f32[3,3,128,128]{3,2,1,0:T(8,128)}, f32[128,256]{1,0:T(8,128)}, f32[3,3,256,256]{3,2,1,0:T(8,128)})) %all-reduce.3.cloned.1.call-update) | async-done | bytes 3080208 | tf_op jit(solution)/shard_map/psum | solution.py:139
  214.0 0.7 copy.31
  214.8 1.9 copy.32
  216.7 0.7 copy.33
  217.3 3.2 %copy.34 = f32[3,3,256,256]{3,2,1,0:T(8,128)} copy(f32[3,3,256,256]{3,2,1,0:T(8,128)} %get-tuple-element.63) | data formatting | bytes 4718592
  (88 shorter events, 15.9 us)
Async XLA Ops:
  7.2 23.0 %copy-start = (bf16[128,256]{1,0:T(8,128)(2,1)S(1)}, bf16[128,256]{1,0:T(8,128)(2,1)}, u32[]{:S(2)}) copy-start(bf16[128,256]{1,0:T(8,128)(2,1)} %param.7) | copy-start | bytes 196612
  7.2 15.6 %copy-start.5 = (bf16[3,3,128,128]{3,2,1,0:T(8,128)(2,1)S(1)}, bf16[3,3,128,128]{3,2,1,0:T(8,128)(2,1)}, u32[]{:S(2)}) copy-start(bf16[3,3,128,128]{3,2,1,0:T(8,128)(2,1)} %param.6) | copy-start | bytes 884740
  7.2 206.9 %all-reduce.3.cloned.1.call-start = ((), (), s32[]{:S(2)}) async-start(), calls=%async_computation | async-start | bytes 6160384 | tf_op jit(solution)/shard_map/psum | solution.py:139
  8.0 3.7 %collective-permute-start = (bf16[1,64,128]{2,1,0:T(8,128)(2,1)S(1)}, bf16[1,64,128]{2,1,0:T(8,128)(2,1)S(1)}, u32[]{:S(2)}, u32[]{:S(2)}) collective-permute-start(bf16[1,64,128]{2,1,0:T(8,128)(2,1)S(1)} %get-tuple-element.21), channel_id=1, source_target_pairs={{0,4},{4,8},{8,12},{1,5},{5,9},{9,13},{2,6},{6,10},{10,14},{3,7},{... | collective-permute-start | bytes 49160 | tf_op jit(solution)/shard_map/ppermute | solution.py:14
  10.4 5.2 %collective-permute-start.1 = (bf16[1,64,128]{2,1,0:T(8,128)(2,1)S(1)}, bf16[1,64,128]{2,1,0:T(8,128)(2,1)S(1)}, u32[]{:S(2)}, u32[]{:S(2)}) collective-permute-start(bf16[1,64,128]{2,1,0:T(8,128)(2,1)S(1)} %get-tuple-element.22), channel_id=1, source_target_pairs={{4,0},{8,4},{12,8},{5,1},{9,5},{13,9},{6,2},{10,6},{14,10},{7,3},{... | collective-permute-start | bytes 49160 | tf_op jit(solution)/shard_map/ppermute | solution.py:15
  16.5 6.5 %collective-permute-start.2 = (bf16[34,1,128]{2,1,0:T(2,128)(2,1)S(1)}, bf16[34,1,128]{2,1,0:T(2,128)(2,1)S(1)}, u32[]{:S(2)}, u32[]{:S(2)}) collective-permute-start(bf16[34,1,128]{2,1,0:T(2,128)(2,1)S(1)} %get-tuple-element.15), channel_id=1, source_target_pairs={{0,1},{1,2},{2,3},{4,5},{5,6},{6,7},{8,9},{9,10},{10,11},{12,13},{... | collective-permute-start | bytes 26120 | tf_op jit(solution)/shard_map/ppermute | solution.py:14
  20.0 5.8 %copy-start.1 = (bf16[1,32,64,128]{3,2,1,0:T(8,128)(2,1)S(1)}, bf16[1,32,64,128]{3,2,1,0:T(8,128)(2,1)}, u32[]{:S(2)}) copy-start(bf16[1,32,64,128]{3,2,1,0:T(8,128)(2,1)} %param.5) | copy-start | bytes 1572868
  20.0 5.8 %collective-permute-start.3 = (bf16[34,1,128]{2,1,0:T(2,128)(2,1)S(1)}, bf16[34,1,128]{2,1,0:T(2,128)(2,1)S(1)}, u32[]{:S(2)}, u32[]{:S(2)}) collective-permute-start(bf16[34,1,128]{2,1,0:T(2,128)(2,1)S(1)} %get-tuple-element.16), channel_id=1, source_target_pairs={{1,0},{2,1},{3,2},{5,4},{6,5},{7,6},{9,8},{10,9},{11,10},{13,12},{... | collective-permute-start | bytes 26120 | tf_op jit(solution)/shard_map/ppermute | solution.py:15
  29.2 5.4 %copy-start.7 = (bf16[1,16,32,256]{3,2,1,0:T(8,128)(2,1)S(1)}, bf16[1,16,32,256]{3,2,1,0:T(8,128)(2,1)}, u32[]{:S(2)}) copy-start(bf16[1,16,32,256]{3,2,1,0:T(8,128)(2,1)} %param.9) | copy-start | bytes 786436
  29.3 13.0 %copy-start.2 = (bf16[3,3,256,256]{3,2,1,0:T(8,128)(2,1)S(1)}, bf16[3,3,256,256]{3,2,1,0:T(8,128)(2,1)}, u32[]{:S(2)}) copy-start(bf16[3,3,256,256]{3,2,1,0:T(8,128)(2,1)} %param.8) | copy-start | bytes 3538948
  30.4 5.9 %collective-permute-start.4 = (bf16[1,32,256]{2,1,0:T(8,128)(2,1)S(1)}, bf16[1,32,256]{2,1,0:T(8,128)(2,1)S(1)}, u32[]{:S(2)}, u32[]{:S(2)}) collective-permute-start(bf16[1,32,256]{2,1,0:T(8,128)(2,1)S(1)} %get-tuple-element.49), channel_id=1, source_target_pairs={{0,4},{4,8},{8,12},{1,5},{5,9},{9,13},{2,6},{6,10},{10,14},{3,7},{... | collective-permute-start | bytes 49160 | tf_op jit(solution)/shard_map/ppermute | solution.py:14
  33.4 4.0 %collective-permute-start.5 = (bf16[1,32,256]{2,1,0:T(8,128)(2,1)S(1)}, bf16[1,32,256]{2,1,0:T(8,128)(2,1)S(1)}, u32[]{:S(2)}, u32[]{:S(2)}) collective-permute-start(bf16[1,32,256]{2,1,0:T(8,128)(2,1)S(1)} %get-tuple-element.50), channel_id=1, source_target_pairs={{4,0},{8,4},{12,8},{5,1},{9,5},{13,9},{6,2},{10,6},{14,10},{7,3},{... | collective-permute-start | bytes 49160 | tf_op jit(solution)/shard_map/ppermute | solution.py:15
  34.7 14.0 %collective-permute-start.9 = (bf16[16,32,256]{2,1,0:T(8,128)(2,1)S(1)}, bf16[16,32,256]{2,1,0:T(8,128)(2,1)S(1)}, u32[]{:S(2)}, u32[]{:S(2)}) collective-permute-start(bf16[16,32,256]{2,1,0:T(8,128)(2,1)S(1)} %bitcast.331), channel_id=1, source_target_pairs={{0,16},{16,0},{1,17},{17,1},{2,18},{18,2},{3,19},{19,3},{4,20},{20... | collective-permute-start | bytes 786440 | tf_op jit(solution)/shard_map/ppermute | solution.py:27
  37.5 5.1 %collective-permute-start.6 = (bf16[18,1,256]{2,1,0:T(2,128)(2,1)S(1)}, bf16[18,1,256]{2,1,0:T(2,128)(2,1)S(1)}, u32[]{:S(2)}, u32[]{:S(2)}) collective-permute-start(bf16[18,1,256]{2,1,0:T(2,128)(2,1)S(1)} %get-tuple-element.41), channel_id=1, source_target_pairs={{0,1},{1,2},{2,3},{4,5},{5,6},{6,7},{8,9},{9,10},{10,11},{12,13},{... | collective-permute-start | bytes 27656 | tf_op jit(solution)/shard_map/ppermute | solution.py:14
  40.9 5.7 %collective-permute-start.7 = (bf16[18,1,256]{2,1,0:T(2,128)(2,1)S(1)}, bf16[18,1,256]{2,1,0:T(2,128)(2,1)S(1)}, u32[]{:S(2)}, u32[]{:S(2)}) collective-permute-start(bf16[18,1,256]{2,1,0:T(2,128)(2,1)S(1)} %get-tuple-element.42), channel_id=1, source_target_pairs={{1,0},{2,1},{3,2},{5,4},{6,5},{7,6},{9,8},{10,9},{11,10},{13,12},{... | collective-permute-start | bytes 27656 | tf_op jit(solution)/shard_map/ppermute | solution.py:15
  49.4 6.8 %collective-permute-start.10 = (bf16[1,32,256]{2,1,0:T(8,128)(2,1)S(1)}, bf16[1,32,256]{2,1,0:T(8,128)(2,1)S(1)}, u32[]{:S(2)}, u32[]{:S(2)}) collective-permute-start(bf16[1,32,256]{2,1,0:T(8,128)(2,1)S(1)} %get-tuple-element.45), channel_id=1, source_target_pairs={{0,4},{4,8},{8,12},{1,5},{5,9},{9,13},{2,6},{6,10},{10,14},{3,7},{... | collective-permute-start | bytes 49160 | tf_op jit(solution)/shard_map/ppermute | solution.py:14
  52.6 3.9 %collective-permute-start.11 = (bf16[1,32,256]{2,1,0:T(8,128)(2,1)S(1)}, bf16[1,32,256]{2,1,0:T(8,128)(2,1)S(1)}, u32[]{:S(2)}, u32[]{:S(2)}) collective-permute-start(bf16[1,32,256]{2,1,0:T(8,128)(2,1)S(1)} %get-tuple-element.46), channel_id=1, source_target_pairs={{4,0},{8,4},{12,8},{5,1},{9,5},{13,9},{6,2},{10,6},{14,10},{7,3},{... | collective-permute-start | bytes 49160 | tf_op jit(solution)/shard_map/ppermute | solution.py:15
  56.1 7.9 %copy-start.3 = (f32[9,256,256]{2,1,0:T(8,128)}, f32[9,256,256]{2,1,0:T(8,128)S(1)}, u32[]{:S(2)}) copy-start(f32[9,256,256]{2,1,0:T(8,128)S(1)} %fusion.4) | copy-start | bytes 7077892
  56.5 6.3 %collective-permute-start.12 = (bf16[18,1,256]{2,1,0:T(2,128)(2,1)S(1)}, bf16[18,1,256]{2,1,0:T(2,128)(2,1)S(1)}, u32[]{:S(2)}, u32[]{:S(2)}) collective-permute-start(bf16[18,1,256]{2,1,0:T(2,128)(2,1)S(1)} %get-tuple-element.37), channel_id=1, source_target_pairs={{1,0},{2,1},{3,2},{5,4},{6,5},{7,6},{9,8},{10,9},{11,10},{13,12},{... | collective-permute-start | bytes 27656 | tf_op jit(solution)/shard_map/ppermute | solution.py:15
  57.8 6.0 %collective-permute-start.13 = (bf16[18,1,256]{2,1,0:T(2,128)(2,1)S(1)}, bf16[18,1,256]{2,1,0:T(2,128)(2,1)S(1)}, u32[]{:S(2)}, u32[]{:S(2)}) collective-permute-start(bf16[18,1,256]{2,1,0:T(2,128)(2,1)S(1)} %get-tuple-element.38), channel_id=1, source_target_pairs={{0,1},{1,2},{2,3},{4,5},{5,6},{6,7},{8,9},{9,10},{10,11},{12,13},{... | collective-permute-start | bytes 27656 | tf_op jit(solution)/shard_map/ppermute | solution.py:14
  71.6 0.8 copy-start.4
  72.5 8.9 %collective-permute-start.8 = (bf16[16,32,256]{2,1,0:T(8,128)(2,1)S(1)}, bf16[16,32,256]{2,1,0:T(8,128)(2,1)S(1)}, u32[]{:S(2)}, u32[]{:S(2)}) collective-permute-start(bf16[16,32,256]{2,1,0:T(8,128)(2,1)S(1)} %bitcast.332), channel_id=1, source_target_pairs={{0,16},{16,0},{1,17},{17,1},{2,18},{18,2},{3,19},{19,3},{4,20},{20... | collective-permute-start | bytes 786440 | tf_op jit(solution)/shard_map/ppermute | solution.py:27
  214.0 2.6 %copy-start.6 = (f32[128,256]{1,0:T(8,128)S(1)}, f32[128,256]{1,0:T(8,128)}, u32[]{:S(2)}) copy-start(f32[128,256]{1,0:T(8,128)} %get-tuple-element.62) | copy-start | bytes 393220
Sparse Core Ops, SparseCore 0:
  72.6 141.4 all-reduce.2
where the time goes:
time: 228 us; the launch traced here: 227 us
  waiting for transfers between devices  153 us (67%)
  starting transfers between devices  31.2 us (14%)
  between operations  14.7 us (6%)
  matrix products  14.2 us (6%)
  local copies, waits for them, and re-layouts  9.64 us (4%)
  other arithmetic  4.38 us (2%)
    psum x1, waiting for transfers between devices, per_device(): lax.psum((grad_first, grad_projection, grad_second), ('section', 'gy', 'g...  133 us
    ppermute x6, starting transfers between devices, padded_2(): before = lax.ppermute(last, axis, up)  20.3 us
    ppermute x6, waiting for transfers between devices, padded_2(): after = lax.ppermute(initial, axis, down)  12.2 us
    ppermute x6, starting transfers between devices, padded_2(): after = lax.ppermute(initial, axis, down)  7.88 us
    ppermute x2, waiting for transfers between devices, from_partner(): return lax.ppermute(block, axis, route)  7.47 us
    unnamed x20, local copies, waits for them, and re-layouts  7.35 us
    dot_general x18, matrix products, conv_slopes(): jnp.einsum('pc,pd->cd', piece, slope, preferred_element_type=jnp.float32)  5.6 us
    dot_general x18, matrix products, conv_forward(): jnp.dot(piece, kernel[row_tap, col_tap], preferred_element_type=jnp.float32)  4.91 us
  transfers between devices with their start and end apart: 15, of which 8 were waited for; matrix products, arithmetic and copies ran while one was open for 3% of the time, Pallas kernels for 0%

commit v1 on v0

--- a/solution.py
+++ b/solution.py
@@ -137,7 +137,7 @@
     output = from_partner(output, "section", 0)
     grad_first = first_back(padded, before, pooled_slope)
     grad_first, grad_projection, grad_second = lax.psum(
-        (grad_first, grad_projection, grad_second), ("section", "gy", "gx")
+        lax.psum((grad_first, grad_projection, grad_second), "section"), ("gy", "gx")
     )
     return (output[None], grad_first, grad_projection, grad_second)
 

time: 228 us -> 282 us (1.24)
  waiting for transfers between devices: 153 us -> 208 us
    psum x1 -> x2, waiting for transfers between devices: 133 us -> 187 us  [the longest x1 100 us: per_device(): lax.psum(lax.psum((grad_first, grad_projection, grad_second), 'section'),...]
  transfers between devices with their start and end apart: 15 -> 16, of which waited for: 8 -> 9; matrix products, arithmetic and copies ran while one was open for 3% -> 2% of each run, Pallas kernels for 0% -> 0%
where the time goes in v1:
time: 282 us; the launch traced here: 281 us
  waiting for transfers between devices  208 us (74%)
  starting transfers between devices  30.2 us (11%)
  between operations  14.7 us (5%)
  matrix products  14.2 us (5%)
  local copies, waits for them, and re-layouts  9.64 us (3%)
  other arithmetic  4.4 us (2%)
    psum x1, waiting for transfers between devices, per_device(): lax.psum(lax.psum((grad_first, grad_projection, grad_second), 'section'),...  100 us
    psum x1, waiting for transfers between devices, per_device(): lax.psum((grad_first, grad_projection, grad_second), 'section')  87.1 us
    ppermute x6, starting transfers between devices, padded_2(): before = lax.ppermute(last, axis, up)  20.3 us
    ppermute x6, waiting for transfers between devices, padded_2(): after = lax.ppermute(initial, axis, down)  12.2 us
    ppermute x6, starting transfers between devices, padded_2(): after = lax.ppermute(initial, axis, down)  7.88 us
    ppermute x2, waiting for transfers between devices, from_partner(): return lax.ppermute(block, axis, route)  7.53 us
    unnamed x20, local copies, waits for them, and re-layouts  7.35 us
  transfers between devices with their start and end apart: 16, of which 9 were waited for; matrix products, arithmetic and copies ran while one was open for 2% of the time, Pallas kernels for 0%

profile of v1, /device:TPU:0, one launch (start us, length us, event | category | flops | bytes accessed | tf_op | source)
XLA Modules:
  0.0 281.3 jit_solution(14978144099598910813)
XLA Ops:
  7.2 0.8 slice_bitcast_fusion.5
  8.0 2.4 collective-permute-start
  10.4 1.3 collective-permute-start.1
  11.7 3.9 %collective-permute-done.1 = bf16[1,64,128]{2,1,0:T(8,128)(2,1)S(1)} collective-permute-done((bf16[1,64,128]{2,1,0:T(8,128)(2,1)S(1)}, bf16[1,64,128]{2,1,0:T(8,128)(2,1)S(1)}, u32[]{:S(2)}, u32[]{:S(2)}) %collective-permute-start.1) | collective-permute-done | bytes 16416 | tf_op jit(solution)/shard_map/ppermute | solution.py:15
  15.6 0.9 pad_maximum_fusion.17
  16.5 3.5 %collective-permute-start.2 = (bf16[34,1,128]{2,1,0:T(2,128)(2,1)S(1)}, bf16[34,1,128]{2,1,0:T(2,128)(2,1)S(1)}, u32[]{:S(2)}, u32[]{:S(2)}) collective-permute-start(bf16[34,1,128]{2,1,0:T(2,128)(2,1)S(1)} %get-tuple-element.18), channel_id=1, source_target_pairs={{0,1},{1,2},{2,3},{4,5},{5,6},{6,7},{8,9},{9,10},{10,11},{12,13},{... | collective-permute-start | bytes 26120 | tf_op jit(solution)/shard_map/ppermute | solution.py:14
  20.0 1.4 collective-permute-start.3
  21.5 1.3 pad_maximum_fusion.1
  23.1 2.7 collective-permute-done.3
  26.2 0.6 fusion.85
  29.3 0.9 convert_reduce_fusion
  30.4 3.0 %collective-permute-start.4 = (bf16[1,32,256]{2,1,0:T(8,128)(2,1)S(1)}, bf16[1,32,256]{2,1,0:T(8,128)(2,1)S(1)}, u32[]{:S(2)}, u32[]{:S(2)}) collective-permute-start(bf16[1,32,256]{2,1,0:T(8,128)(2,1)S(1)} %get-tuple-element.52), channel_id=1, source_target_pairs={{0,4},{4,8},{8,12},{1,5},{5,9},{9,13},{2,6},{6,10},{10,14},{3,7},{... | collective-permute-start | bytes 49160 | tf_op jit(solution)/shard_map/ppermute | solution.py:14
  33.4 1.3 collective-permute-start.5
  34.7 1.6 collective-permute-start.9
  36.3 1.2 collective-permute-done.5
  37.5 3.5 %collective-permute-start.6 = (bf16[18,1,256]{2,1,0:T(2,128)(2,1)S(1)}, bf16[18,1,256]{2,1,0:T(2,128)(2,1)S(1)}, u32[]{:S(2)}, u32[]{:S(2)}) collective-permute-start(bf16[18,1,256]{2,1,0:T(2,128)(2,1)S(1)} %get-tuple-element.44), channel_id=1, source_target_pairs={{0,1},{1,2},{2,3},{4,5},{5,6},{6,7},{8,9},{9,10},{10,11},{12,13},{... | collective-permute-start | bytes 27656 | tf_op jit(solution)/shard_map/ppermute | solution.py:14
  40.9 1.3 collective-permute-start.7
  42.5 4.1 %collective-permute-done.7 = bf16[18,1,256]{2,1,0:T(2,128)(2,1)S(1)} collective-permute-done((bf16[18,1,256]{2,1,0:T(2,128)(2,1)S(1)}, bf16[18,1,256]{2,1,0:T(2,128)(2,1)S(1)}, u32[]{:S(2)}, u32[]{:S(2)}) %collective-permute-start.7) | collective-permute-done | bytes 9248 | tf_op jit(solution)/shard_map/ppermute | solution.py:15
  49.4 3.2 %collective-permute-start.10 = (bf16[1,32,256]{2,1,0:T(8,128)(2,1)S(1)}, bf16[1,32,256]{2,1,0:T(8,128)(2,1)S(1)}, u32[]{:S(2)}, u32[]{:S(2)}) collective-permute-start(bf16[1,32,256]{2,1,0:T(8,128)(2,1)S(1)} %get-tuple-element.48), channel_id=1, source_target_pairs={{0,4},{4,8},{8,12},{1,5},{5,9},{9,13},{2,6},{6,10},{10,14},{3,7},{... | collective-permute-start | bytes 49160 | tf_op jit(solution)/shard_map/ppermute | solution.py:14
  52.6 1.3 collective-permute-start.11
  56.5 1.3 collective-permute-start.12
  57.8 4.7 %collective-permute-start.13 = (bf16[18,1,256]{2,1,0:T(2,128)(2,1)S(1)}, bf16[18,1,256]{2,1,0:T(2,128)(2,1)S(1)}, u32[]{:S(2)}, u32[]{:S(2)}) collective-permute-start(bf16[18,1,256]{2,1,0:T(2,128)(2,1)S(1)} %get-tuple-element.41), channel_id=1, source_target_pairs={{0,1},{1,2},{2,3},{4,5},{5,6},{6,7},{8,9},{9,10},{10,11},{12,13},{... | collective-permute-start | bytes 27656 | tf_op jit(solution)/shard_map/ppermute | solution.py:14
  62.9 0.9 collective-permute-done.13
  66.4 0.9 fusion.91
  71.6 0.8 copy-done.4
  72.5 87.1 %all-reduce.7.cloned.1.call-done = (f32[3,3,128,128]{3,2,1,0:T(8,128)}, f32[128,256]{1,0:T(8,128)}, f32[3,3,256,256]{3,2,1,0:T(8,128)}) async-done(((f32[3,3,128,128]{3,2,1,0:T(8,128)}, f32[128,256]{1,0:T(8,128)}, f32[3,3,256,256]{3,2,1,0:T(8,128)}), (f32[3,3,128,128]{3,2,1,0:T(8,128)}, f32[128,256]{1,0:T(8,128)}, f32[3,3,256,256]{3,2,1,0:T(8,128)})) %all-reduce.7.cloned.1.call-update) | async-done | bytes 3080208 | tf_op jit(solution)/shard_map/psum | solution.py:140
  160.1 7.5 %collective-permute-done.8 = bf16[16,32,256]{2,1,0:T(8,128)(2,1)S(1)} collective-permute-done((bf16[16,32,256]{2,1,0:T(8,128)(2,1)S(1)}, bf16[16,32,256]{2,1,0:T(8,128)(2,1)S(1)}, u32[]{:S(2)}, u32[]{:S(2)}) %collective-permute-start.8) | collective-permute-done | bytes 262176 | tf_op jit(solution)/shard_map/ppermute | solution.py:27
  167.6 100.3 %all-reduce.5.cloned.1.call-done = (f32[3,3,128,128]{3,2,1,0:T(8,128)}, f32[128,256]{1,0:T(8,128)}, f32[3,3,256,256]{3,2,1,0:T(8,128)}) async-done(((f32[3,3,128,128]{3,2,1,0:T(8,128)}, f32[128,256]{1,0:T(8,128)}, f32[3,3,256,256]{3,2,1,0:T(8,128)}), (f32[3,3,128,128]{3,2,1,0:T(8,128)}, f32[128,256]{1,0:T(8,128)}, f32[3,3,256,256]{3,2,1,0:T(8,128)})) %all-reduce.5.cloned.1.call-update) | async-done | bytes 3080208 | tf_op jit(solution)/shard_map/psum | solution.py:139
  267.9 0.7 copy.34
  268.6 1.9 copy.35
  270.6 0.7 copy.36
  271.2 3.2 %copy.37 = f32[3,3,256,256]{3,2,1,0:T(8,128)} copy(f32[3,3,256,256]{3,2,1,0:T(8,128)} %get-tuple-element.66) | data formatting | bytes 4718592
  (91 shorter events, 16.4 us)
Async XLA Ops:
  7.2 23.0 %copy-start = (bf16[128,256]{1,0:T(8,128)(2,1)S(1)}, bf16[128,256]{1,0:T(8,128)(2,1)}, u32[]{:S(2)}) copy-start(bf16[128,256]{1,0:T(8,128)(2,1)} %param.7) | copy-start | bytes 196612
  7.2 15.6 %copy-start.5 = (bf16[3,3,128,128]{3,2,1,0:T(8,128)(2,1)S(1)}, bf16[3,3,128,128]{3,2,1,0:T(8,128)(2,1)}, u32[]{:S(2)}) copy-start(bf16[3,3,128,128]{3,2,1,0:T(8,128)(2,1)} %param.6) | copy-start | bytes 884740
  7.2 152.4 %all-reduce.7.cloned.1.call-start = ((), (), s32[]{:S(2)}) async-start(), calls=%async_computation.1 | async-start | bytes 6160384 | tf_op jit(solution)/shard_map/psum | solution.py:140
  8.0 3.7 %collective-permute-start = (bf16[1,64,128]{2,1,0:T(8,128)(2,1)S(1)}, bf16[1,64,128]{2,1,0:T(8,128)(2,1)S(1)}, u32[]{:S(2)}, u32[]{:S(2)}) collective-permute-start(bf16[1,64,128]{2,1,0:T(8,128)(2,1)S(1)} %get-tuple-element.24), channel_id=1, source_target_pairs={{0,4},{4,8},{8,12},{1,5},{5,9},{9,13},{2,6},{6,10},{10,14},{3,7},{... | collective-permute-start | bytes 49160 | tf_op jit(solution)/shard_map/ppermute | solution.py:14
  10.4 5.2 %collective-permute-start.1 = (bf16[1,64,128]{2,1,0:T(8,128)(2,1)S(1)}, bf16[1,64,128]{2,1,0:T(8,128)(2,1)S(1)}, u32[]{:S(2)}, u32[]{:S(2)}) collective-permute-start(bf16[1,64,128]{2,1,0:T(8,128)(2,1)S(1)} %get-tuple-element.25), channel_id=1, source_target_pairs={{4,0},{8,4},{12,8},{5,1},{9,5},{13,9},{6,2},{10,6},{14,10},{7,3},{... | collective-permute-start | bytes 49160 | tf_op jit(solution)/shard_map/ppermute | solution.py:15
  16.5 6.5 %collective-permute-start.2 = (bf16[34,1,128]{2,1,0:T(2,128)(2,1)S(1)}, bf16[34,1,128]{2,1,0:T(2,128)(2,1)S(1)}, u32[]{:S(2)}, u32[]{:S(2)}) collective-permute-start(bf16[34,1,128]{2,1,0:T(2,128)(2,1)S(1)} %get-tuple-element.18), channel_id=1, source_target_pairs={{0,1},{1,2},{2,3},{4,5},{5,6},{6,7},{8,9},{9,10},{10,11},{12,13},{... | collective-permute-start | bytes 26120 | tf_op jit(solution)/shard_map/ppermute | solution.py:14
  20.0 5.8 %copy-start.1 = (bf16[1,32,64,128]{3,2,1,0:T(8,128)(2,1)S(1)}, bf16[1,32,64,128]{3,2,1,0:T(8,128)(2,1)}, u32[]{:S(2)}) copy-start(bf16[1,32,64,128]{3,2,1,0:T(8,128)(2,1)} %param.5) | copy-start | bytes 1572868
  20.0 5.8 %collective-permute-start.3 = (bf16[34,1,128]{2,1,0:T(2,128)(2,1)S(1)}, bf16[34,1,128]{2,1,0:T(2,128)(2,1)S(1)}, u32[]{:S(2)}, u32[]{:S(2)}) collective-permute-start(bf16[34,1,128]{2,1,0:T(2,128)(2,1)S(1)} %get-tuple-element.19), channel_id=1, source_target_pairs={{1,0},{2,1},{3,2},{5,4},{6,5},{7,6},{9,8},{10,9},{11,10},{13,12},{... | collective-permute-start | bytes 26120 | tf_op jit(solution)/shard_map/ppermute | solution.py:15
  29.2 5.4 %copy-start.7 = (bf16[1,16,32,256]{3,2,1,0:T(8,128)(2,1)S(1)}, bf16[1,16,32,256]{3,2,1,0:T(8,128)(2,1)}, u32[]{:S(2)}) copy-start(bf16[1,16,32,256]{3,2,1,0:T(8,128)(2,1)} %param.9) | copy-start | bytes 786436
  29.3 13.0 %copy-start.2 = (bf16[3,3,256,256]{3,2,1,0:T(8,128)(2,1)S(1)}, bf16[3,3,256,256]{3,2,1,0:T(8,128)(2,1)}, u32[]{:S(2)}) copy-start(bf16[3,3,256,256]{3,2,1,0:T(8,128)(2,1)} %param.8) | copy-start | bytes 3538948
  30.4 5.9 %collective-permute-start.4 = (bf16[1,32,256]{2,1,0:T(8,128)(2,1)S(1)}, bf16[1,32,256]{2,1,0:T(8,128)(2,1)S(1)}, u32[]{:S(2)}, u32[]{:S(2)}) collective-permute-start(bf16[1,32,256]{2,1,0:T(8,128)(2,1)S(1)} %get-tuple-element.52), channel_id=1, source_target_pairs={{0,4},{4,8},{8,12},{1,5},{5,9},{9,13},{2,6},{6,10},{10,14},{3,7},{... | collective-permute-start | bytes 49160 | tf_op jit(solution)/shard_map/ppermute | solution.py:14
  33.4 4.0 %collective-permute-start.5 = (bf16[1,32,256]{2,1,0:T(8,128)(2,1)S(1)}, bf16[1,32,256]{2,1,0:T(8,128)(2,1)S(1)}, u32[]{:S(2)}, u32[]{:S(2)}) collective-permute-start(bf16[1,32,256]{2,1,0:T(8,128)(2,1)S(1)} %get-tuple-element.53), channel_id=1, source_target_pairs={{4,0},{8,4},{12,8},{5,1},{9,5},{13,9},{6,2},{10,6},{14,10},{7,3},{... | collective-permute-start | bytes 49160 | tf_op jit(solution)/shard_map/ppermute | solution.py:15
  34.7 14.0 %collective-permute-start.9 = (bf16[16,32,256]{2,1,0:T(8,128)(2,1)S(1)}, bf16[16,32,256]{2,1,0:T(8,128)(2,1)S(1)}, u32[]{:S(2)}, u32[]{:S(2)}) collective-permute-start(bf16[16,32,256]{2,1,0:T(8,128)(2,1)S(1)} %bitcast.331), channel_id=1, source_target_pairs={{0,16},{16,0},{1,17},{17,1},{2,18},{18,2},{3,19},{19,3},{4,20},{20... | collective-permute-start | bytes 786440 | tf_op jit(solution)/shard_map/ppermute | solution.py:27
  37.5 5.1 %collective-permute-start.6 = (bf16[18,1,256]{2,1,0:T(2,128)(2,1)S(1)}, bf16[18,1,256]{2,1,0:T(2,128)(2,1)S(1)}, u32[]{:S(2)}, u32[]{:S(2)}) collective-permute-start(bf16[18,1,256]{2,1,0:T(2,128)(2,1)S(1)} %get-tuple-element.44), channel_id=1, source_target_pairs={{0,1},{1,2},{2,3},{4,5},{5,6},{6,7},{8,9},{9,10},{10,11},{12,13},{... | collective-permute-start | bytes 27656 | tf_op jit(solution)/shard_map/ppermute | solution.py:14
  40.9 5.7 %collective-permute-start.7 = (bf16[18,1,256]{2,1,0:T(2,128)(2,1)S(1)}, bf16[18,1,256]{2,1,0:T(2,128)(2,1)S(1)}, u32[]{:S(2)}, u32[]{:S(2)}) collective-permute-start(bf16[18,1,256]{2,1,0:T(2,128)(2,1)S(1)} %get-tuple-element.45), channel_id=1, source_target_pairs={{1,0},{2,1},{3,2},{5,4},{6,5},{7,6},{9,8},{10,9},{11,10},{13,12},{... | collective-permute-start | bytes 27656 | tf_op jit(solution)/shard_map/ppermute | solution.py:15
  49.4 6.8 %collective-permute-start.10 = (bf16[1,32,256]{2,1,0:T(8,128)(2,1)S(1)}, bf16[1,32,256]{2,1,0:T(8,128)(2,1)S(1)}, u32[]{:S(2)}, u32[]{:S(2)}) collective-permute-start(bf16[1,32,256]{2,1,0:T(8,128)(2,1)S(1)} %get-tuple-element.48), channel_id=1, source_target_pairs={{0,4},{4,8},{8,12},{1,5},{5,9},{9,13},{2,6},{6,10},{10,14},{3,7},{... | collective-permute-start | bytes 49160 | tf_op jit(solution)/shard_map/ppermute | solution.py:14
  52.6 3.9 %collective-permute-start.11 = (bf16[1,32,256]{2,1,0:T(8,128)(2,1)S(1)}, bf16[1,32,256]{2,1,0:T(8,128)(2,1)S(1)}, u32[]{:S(2)}, u32[]{:S(2)}) collective-permute-start(bf16[1,32,256]{2,1,0:T(8,128)(2,1)S(1)} %get-tuple-element.49), channel_id=1, source_target_pairs={{4,0},{8,4},{12,8},{5,1},{9,5},{13,9},{6,2},{10,6},{14,10},{7,3},{... | collective-permute-start | bytes 49160 | tf_op jit(solution)/shard_map/ppermute | solution.py:15
  56.1 7.9 %copy-start.3 = (f32[9,256,256]{2,1,0:T(8,128)}, f32[9,256,256]{2,1,0:T(8,128)S(1)}, u32[]{:S(2)}) copy-start(f32[9,256,256]{2,1,0:T(8,128)S(1)} %fusion.4) | copy-start | bytes 7077892
  56.5 6.3 %collective-permute-start.12 = (bf16[18,1,256]{2,1,0:T(2,128)(2,1)S(1)}, bf16[18,1,256]{2,1,0:T(2,128)(2,1)S(1)}, u32[]{:S(2)}, u32[]{:S(2)}) collective-permute-start(bf16[18,1,256]{2,1,0:T(2,128)(2,1)S(1)} %get-tuple-element.40), channel_id=1, source_target_pairs={{1,0},{2,1},{3,2},{5,4},{6,5},{7,6},{9,8},{10,9},{11,10},{13,12},{... | collective-permute-start | bytes 27656 | tf_op jit(solution)/shard_map/ppermute | solution.py:15
  57.8 6.0 %collective-permute-start.13 = (bf16[18,1,256]{2,1,0:T(2,128)(2,1)S(1)}, bf16[18,1,256]{2,1,0:T(2,128)(2,1)S(1)}, u32[]{:S(2)}, u32[]{:S(2)}) collective-permute-start(bf16[18,1,256]{2,1,0:T(2,128)(2,1)S(1)} %get-tuple-element.41), channel_id=1, source_target_pairs={{0,1},{1,2},{2,3},{4,5},{5,6},{6,7},{8,9},{9,10},{10,11},{12,13},{... | collective-permute-start | bytes 27656 | tf_op jit(solution)/shard_map/ppermute | solution.py:14
  71.6 0.8 copy-start.4
  72.5 195.5 %all-reduce.5.cloned.1.call-start = ((), (), s32[]{:S(2)}) async-start(), calls=%async_computation | async-start | bytes 6160384 | tf_op jit(solution)/shard_map/psum | solution.py:139
  159.7 7.9 %collective-permute-start.8 = (bf16[16,32,256]{2,1,0:T(8,128)(2,1)S(1)}, bf16[16,32,256]{2,1,0:T(8,128)(2,1)S(1)}, u32[]{:S(2)}, u32[]{:S(2)}) collective-permute-start(bf16[16,32,256]{2,1,0:T(8,128)(2,1)S(1)} %bitcast.332), channel_id=1, source_target_pairs={{0,16},{16,0},{1,17},{17,1},{2,18},{18,2},{3,19},{19,3},{4,20},{20... | collective-permute-start | bytes 786440 | tf_op jit(solution)/shard_map/ppermute | solution.py:27
  267.9 2.6 copy-start.6
Sparse Core Ops, SparseCore 0:
  72.6 86.9 all-reduce.6
  163.5 104.3 all-reduce.4
